TPU v7x, 256 devices: a whole 4x4x8 slice. The times are simulated.
256 devices in a mesh: seq: 8 (over y, core), batch: 32 (over x, z).
Axes of the slice: x: 4, y: 4, z: 8, core: 2. Of those that a mesh axis runs over, the one named last changes fastest.
Arguments:
- hidden: bfloat16 [32, 3072, 1024], P('batch', 'seq'), may hold values from -6 to 6
- grad_out: bfloat16 [32, 3072, 1024], P('batch', 'seq'), may hold values from -6 to 6
- block_offsets: int32 [32, 16, 24, 4], P('batch', 'seq'), may hold values from 0 to 23, as said below
- w_query: bfloat16 [1024, 1024], replicated, may hold values from -0.1875 to 0.1875
- w_key: bfloat16 [1024, 1024], replicated, may hold values from -0.1875 to 0.1875
- w_value: bfloat16 [1024, 1024], replicated, may hold values from -0.1875 to 0.1875
- w_out: bfloat16 [1024, 1024], replicated, may hold values from -0.1875 to 0.1875
Outputs:
- grad_hidden: bfloat16 [32, 3072, 1024], P('batch', 'seq')
- grad_weights: float32 [4, 1024, 1024], P(None, 'batch', 'seq')
Inputs may be any that keep to these rules, and one draw needn't show every extreme that they name: `block_offsets`: slot 0 of every list is 0 (the query's own block); the other slots of a list hold distinct values from 1 to 23, and a value greater than the query block's index leaves its slot empty.
All inputs are finite; a program needn't handle non-finite values.
Results may differ from a plain program's by a relative error of at most 0.012.
Values may be sent and summed in bfloat16 or wider, within the bound.
A program may use at most 128 MiB of HBM per device.

v0:
```python
import math

import jax
import jax.numpy as jnp
from jax import lax
from jax.sharding import Mesh
from jax.sharding import PartitionSpec as P

BLK = 128
BATCH = ("batch_0", "batch_1")
SEQ = ("seq_0", "seq_1")


def sum_by_axis(subtotal, axes):
    for axis in axes:
        subtotal = lax.psum_scatter(subtotal, axis, scatter_dimension=0, tiled=True)
    return subtotal


def split_up(x, dim, devices):
    before, after = (x.shape[:dim], x.shape[dim + 1 :])
    return jnp.moveaxis(x.reshape(*before, devices, -1, *after), dim, 0)


def sum_at_owner(x, axis, dim):
    devices = lax.axis_size(axis)
    parts = lax.all_to_all(split_up(x, dim, devices), axis, 0, 0, tiled=True)
    return jnp.sum(parts, axis=0)


def in_order(parts, dim):
    parts = jnp.moveaxis(parts, 0, dim)
    shape = parts.shape
    return parts.reshape(*shape[:dim], shape[dim] * shape[dim + 1], *shape[dim + 2 :])


def all_blocks(x, axes, sequence):
    parts = x[None]
    for k in sequence:
        parts = lax.all_gather(parts, axes[k], axis=0, tiled=True)
    held = [lax.axis_size(axes[k]) for k in reversed(sequence)]
    parts = parts.reshape(*held, *x.shape)
    turned = sorted(range(len(sequence)), key=lambda place: sequence[len(sequence) - 1 - place])
    return parts.transpose(*turned, *range(len(sequence), parts.ndim)).reshape(-1, *x.shape)


def whole_of(x, axes, sequence, dim):
    return in_order(all_blocks(x, axes, sequence), dim)


def sent_and_summed(x, axis, dim):
    parts = split_up(x, dim, lax.axis_size(axis))
    arrived = lax.all_to_all(parts, axis, split_axis=0, concat_axis=0, tiled=True)
    return arrived.astype(jnp.float32).sum(axis=0)


def pick_blocks(source, chosen):
    return source[chosen]


def add_blocks(running, chosen, portion):
    return running.at[chosen].add(portion)


def scatter_blocks(running, block_ids, portion):
    heads_n = portion.shape[0]
    flat_ids = block_ids.reshape(heads_n, -1)
    flat_part = portion.reshape((heads_n, -1) + portion.shape[3:])
    return jax.vmap(add_blocks)(running, flat_ids, flat_part)


def times_transposed(matrix, weight):
    return lax.dot_general(
        matrix, weight, (((1,), (1,)), ((), ())), preferred_element_type=jnp.float32
    )


def inner_rows(left_side, right_side):
    return lax.dot_general(
        left_side, right_side, (((0,), (0,)), ((), ())), preferred_element_type=jnp.float32
    )


def attend_group(queries, key_all, value_all, out_grads, offsets, first_block):
    group_len = queries.shape[1]
    block_len = queries.shape[2]
    score_scale = 1.0 / math.sqrt(queries.shape[3])
    query_block = first_block + jnp.arange(group_len, dtype=jnp.int32)
    usable = offsets <= query_block[None, :, None]
    block_ids = jnp.where(usable, query_block[None, :, None] - offsets, 0)
    picked_keys = jax.vmap(pick_blocks)(key_all, block_ids)
    picked_values = jax.vmap(pick_blocks)(value_all, block_ids)
    scores = (
        jnp.einsum("hgqd,hgnkd->hgqnk", queries, picked_keys, preferred_element_type=jnp.float32)
        * score_scale
    )
    within = jnp.arange(block_len, dtype=jnp.int32)
    query_pos = query_block[:, None] * block_len + within[None, :]
    key_pos = block_ids[..., None] * block_len + within
    allowed = usable[:, :, None, :, None] & (
        key_pos[:, :, None, :, :] <= query_pos[None, :, :, None, None]
    )
    row_top = jnp.max(jnp.where(allowed, scores, -jnp.inf), axis=(3, 4), keepdims=True)
    raised = jnp.where(allowed, jnp.exp(scores - row_top), 0.0)
    denom_sum = jnp.sum(raised, axis=(3, 4), keepdims=True)
    probabilities = raised / denom_sum
    probs_half = probabilities.astype(jnp.bfloat16)
    attended = jnp.einsum(
        "hgqnk,hgnkd->hgqd", probs_half, picked_values, preferred_element_type=jnp.float32
    ).astype(jnp.bfloat16)
    delta_rows = jnp.sum(out_grads.astype(jnp.float32) * attended.astype(jnp.float32), axis=-1)
    prob_grad = jnp.einsum(
        "hgqd,hgnkd->hgqnk", out_grads, picked_values, preferred_element_type=jnp.float32
    )
    score_grad = (probabilities * (prob_grad - delta_rows[:, :, :, None, None])).astype(
        jnp.bfloat16
    )
    query_grad = (
        jnp.einsum("hgqnk,hgnkd->hgqd", score_grad, picked_keys, preferred_element_type=jnp.float32)
        * score_scale
    ).astype(jnp.bfloat16)
    key_part = (
        jnp.einsum("hgqnk,hgqd->hgnkd", score_grad, queries, preferred_element_type=jnp.float32)
        * score_scale
    )
    value_part = jnp.einsum(
        "hgqnk,hgqd->hgnkd", probs_half, out_grads, preferred_element_type=jnp.float32
    )
    return (attended, query_grad, key_part, value_part, block_ids)


def sharded_terms(factor_pairs, row_block, width):
    pair_count = len(factor_pairs)
    pieces = [inner_rows(left_side, right_side) for left_side, right_side in factor_pairs]
    summed_rows = sum_by_axis(pieces[0], BATCH)
    summed_rows = summed_rows.reshape(row_block, pair_count, width)
    col_block = sum_at_owner(summed_rows, SEQ, 2)
    return col_block.transpose(1, 0, 2)


def per_device(hidden, grad_out, block_offsets, w_query, w_key, w_value, w_out):
    tokens = hidden[0]
    grad_rows = grad_out[0]
    row_count = tokens.shape[0]
    width = tokens.shape[1]
    seq_count = lax.axis_size(SEQ)
    batch_count = lax.axis_size(BATCH)
    queries = jnp.dot(tokens, w_query, preferred_element_type=jnp.float32).astype(jnp.bfloat16)
    key_rows = jnp.dot(tokens, w_key, preferred_element_type=jnp.float32).astype(jnp.bfloat16)
    value_rows = jnp.dot(tokens, w_value, preferred_element_type=jnp.float32).astype(jnp.bfloat16)
    attn_grad = times_transposed(grad_rows, w_out).astype(jnp.bfloat16)
    stacked = jnp.stack([queries, key_rows, value_rows, attn_grad])
    by_heads = lax.all_to_all(stacked, SEQ, split_axis=2, concat_axis=1, tiled=True)
    seq_len = by_heads.shape[1]
    head_width = by_heads.shape[2]
    offsets = block_offsets[0]
    head_count = offsets.shape[0]
    head_size = head_width // head_count
    block_total = seq_len // BLK
    arranged = by_heads.reshape(4, block_total, BLK, head_count, head_size).transpose(0, 3, 1, 2, 4)
    group_len = min(block_total, max(1, 512 // BLK))
    group_count = block_total // group_len

    def grouped(source):
        shaped = source.reshape((source.shape[0], group_count, group_len) + source.shape[2:])
        return jnp.moveaxis(shaped, 1, 0)

    def ungrouped(source):
        moved = jnp.moveaxis(source, 0, 1)
        return moved.reshape((moved.shape[0], block_total) + moved.shape[3:])

    key_all = arranged[1]
    value_all = arranged[2]

    def group_step(running, inputs):
        key_acc, value_acc = running
        query_group, grad_group, offset_group, first_block = inputs
        attended, query_grad, key_part, value_part, block_ids = attend_group(
            query_group, key_all, value_all, grad_group, offset_group, first_block
        )
        key_acc = scatter_blocks(key_acc, block_ids, key_part)
        value_acc = scatter_blocks(value_acc, block_ids, value_part)
        return ((key_acc, value_acc), (attended, query_grad))

    empty = jnp.zeros((head_count, block_total, BLK, head_size), jnp.float32)
    starts = jnp.arange(group_count, dtype=jnp.int32) * group_len
    (key_acc, value_acc), (attended_g, query_g) = lax.scan(
        group_step,
        (empty, empty),
        (grouped(arranged[0]), grouped(arranged[3]), grouped(offsets), starts),
    )
    head_grads = jnp.stack(
        [
            ungrouped(query_g),
            key_acc.astype(jnp.bfloat16),
            value_acc.astype(jnp.bfloat16),
            ungrouped(attended_g),
        ]
    )
    head_grads = head_grads.transpose(0, 2, 3, 1, 4).reshape(4, seq_len, head_width)
    by_tokens = lax.all_to_all(head_grads, SEQ, split_axis=1, concat_axis=2, tiled=True)
    query_tok = by_tokens[0]
    key_tok = by_tokens[1]
    value_tok = by_tokens[2]
    attended_tok = by_tokens[3]
    grad_hidden = (
        times_transposed(query_tok, w_query)
        + times_transposed(key_tok, w_key)
        + times_transposed(value_tok, w_value)
    ).astype(jnp.bfloat16)
    row_block = width // batch_count
    head_factors = head_grads[:3].transpose(1, 0, 2).reshape(seq_len, 3 * head_width)
    col_sums = inner_rows(whole_of(tokens, SEQ, (0, 1), 0), head_factors)
    head_part = sent_and_summed(col_sums.astype(jnp.bfloat16), BATCH, 0)
    head_part = head_part.reshape(row_block, 3, head_width).transpose(1, 0, 2)
    out_part = sharded_terms([(attended_tok, grad_rows)], row_block, width)
    grad_weights = jnp.concatenate([head_part, out_part], axis=0)
    norm_factor = 1.0 / math.sqrt(row_count * seq_count * batch_count)
    return (grad_hidden[None], grad_weights * norm_factor)


def solution(mesh):
    torus = Mesh(mesh.devices.reshape(4, 2, 4, 8), ("seq_0", "seq_1", "batch_0", "batch_1"))
    in_specs = (
        P(BATCH, SEQ, None),
        P(BATCH, SEQ, None),
        P(BATCH, SEQ, None, None),
        P(),
        P(),
        P(),
        P(),
    )
    out_specs = (P(BATCH, SEQ, None), P(None, BATCH, SEQ))
    return jax.shard_map(
        per_device, mesh=torus, in_specs=in_specs, out_specs=out_specs, check_vma=False
    )
```

profile of v0, /device:TPU:1, one launch (start us, length us, event | category | flops | bytes accessed | tf_op | source)
XLA Modules:
  0.0 531.2 jit_solution(656771922350788784)
XLA Ops:
  8.8 3.0 fusion.37
  17.5 6.0 %copy.99 = bf16[4,384,1024]{1,0,2:T(4,128)(2,1)} copy(bf16[4,384,1024]{2,1,0:T(8,128)(2,1)} %pad_maximum_fusion) | data formatting | bytes 6291456 | tf_op jit(solution)/shard_map/stack | solution.py:152
  23.5 7.7 %all-to-all-start = ((bf16[4,384,1024]{1,0,2:T(4,128)(2,1)}), bf16[4,384,1024]{1,0,2:T(4,128)(2,1)}, u32[]{:S(2)}, u32[]{:S(2)}) async-start(bf16[4,384,1024]{1,0,2:T(4,128)(2,1)} %copy.99), calls=%async_computation | async-start | bytes 6291456 | tf_op jit(solution)/shard_map/all_to_all | solution.py:153
  31.3 59.0 %all-to-all-done = bf16[4,384,1024]{1,0,2:T(4,128)(2,1)} async-done(((bf16[4,384,1024]{1,0,2:T(4,128)(2,1)}), bf16[4,384,1024]{1,0,2:T(4,128)(2,1)}, u32[]{:S(2)}, u32[]{:S(2)}) %all-to-all-start) | async-done | bytes 3145760 | tf_op jit(solution)/shard_map/all_to_all | solution.py:153
  90.4 5.4 %copy.145 = bf16[4,384,8,128]{1,2,3,0:T(8,128)(2,1)} copy(bf16[4,384,8,128]{1,0,3,2:T(4,128)(2,1)} %bitcast.27) | data formatting | bytes 6291456 | tf_op jit(solution)/shard_map/all_to_all | solution.py:153
  95.8 5.9 %reshape.213 = bf16[4,24,128,2,64]{2,1,4,3,0:T(8,128)(2,1)} reshape(bf16[4,8,384,128]{2,1,3,0:T(8,128)(2,1)} %bitcast.231) | data formatting | bytes 6291456 | tf_op jit(solution)/shard_map/reshape | solution.py:160
  101.7 3.5 slice_bitcast_fusion
  110.2 2.7 copy_bitcast_fusion.1
  116.0 217.0 %while.16 = (s32[]{:T(128)}, f32[2,24,128,64]{2,3,1,0:T(8,128)}, f32[2,24,128,64]{2,3,1,0:T(8,128)}, bf16[6,2,4,128,64]{3,4,2,0,1:T(8,128)(2,1)}, bf16[6,2,4,128...) while((s32[]{:T(128)}, f32[2,24,128,64]{2,3,1,0:T(8,128)}, ...), condition=%wide.region_6.7_spmd, body=%wide.region_0.6_spmd.sunk | while | flops 421726688 | bytes 44855372 | solution.py:187
  117.9 3.1 gather_fusion
  123.4 2.6 select_reduce_fusion.2
  126.9 3.0 multiply_reduce_fusion.2
  134.4 6.3 %scatter_fusion = f32[2,24,128,64]{2,3,1,0:T(8,128)} fusion(f32[2,24,128,64]{2,3,1,0:T(8,128)} %get-tuple-element.248, s32[32]{0:T(128)S(1)} %reshape.268, f32[32,128,64]{1,2,0:T(8,128)S(1)} %bitcast.223), kind=kCustom, calls=%fused_computation.2.clone.1 | custom fusion | flops 262144 | bytes 3145984 | tf_op jit(solution)/shard_map/while/body/eval_jaxpr/vmap()/scatter-add | solution.py:62
  140.7 3.3 fusion.95
  144.0 6.3 %scatter_fusion.1 = f32[2,24,128,64]{2,3,1,0:T(8,128)} fusion(f32[2,24,128,64]{2,3,1,0:T(8,128)} %get-tuple-element.249, s32[32]{0:T(128)S(1)} %reshape.268, f32[32,128,64]{1,2,0:T(8,128)S(1)} %bitcast.224), kind=kCustom, calls=%fused_computation.3.clone.1 | custom fusion | flops 262144 | bytes 3145984 | tf_op jit(solution)/shard_map/while/body/eval_jaxpr/vmap()/scatter-add | solution.py:62
  151.0 2.7 fusion.96
  155.6 3.1 gather_fusion
  161.1 2.5 select_reduce_fusion.2
  164.5 2.9 multiply_reduce_fusion.2
  172.0 5.7 %scatter_fusion = f32[2,24,128,64]{2,3,1,0:T(8,128)} fusion(f32[2,24,128,64]{2,3,1,0:T(8,128)} %get-tuple-element.248, s32[32]{0:T(128)S(1)} %reshape.268, f32[32,128,64]{1,2,0:T(8,128)S(1)} %bitcast.223), kind=kCustom, calls=%fused_computation.2.clone.1 | custom fusion | flops 262144 | bytes 3145984 | tf_op jit(solution)/shard_map/while/body/eval_jaxpr/vmap()/scatter-add | solution.py:62
  177.8 3.3 fusion.95
  181.0 5.8 %scatter_fusion.1 = f32[2,24,128,64]{2,3,1,0:T(8,128)} fusion(f32[2,24,128,64]{2,3,1,0:T(8,128)} %get-tuple-element.249, s32[32]{0:T(128)S(1)} %reshape.268, f32[32,128,64]{1,2,0:T(8,128)S(1)} %bitcast.224), kind=kCustom, calls=%fused_computation.3.clone.1 | custom fusion | flops 262144 | bytes 3145984 | tf_op jit(solution)/shard_map/while/body/eval_jaxpr/vmap()/scatter-add | solution.py:62
  187.6 2.7 fusion.96
  192.1 3.1 gather_fusion
  197.7 2.5 select_reduce_fusion.2
  201.1 2.9 multiply_reduce_fusion.2
  208.6 5.6 %scatter_fusion = f32[2,24,128,64]{2,3,1,0:T(8,128)} fusion(f32[2,24,128,64]{2,3,1,0:T(8,128)} %get-tuple-element.248, s32[32]{0:T(128)S(1)} %reshape.268, f32[32,128,64]{1,2,0:T(8,128)S(1)} %bitcast.223), kind=kCustom, calls=%fused_computation.2.clone.1 | custom fusion | flops 262144 | bytes 3145984 | tf_op jit(solution)/shard_map/while/body/eval_jaxpr/vmap()/scatter-add | solution.py:62
  214.2 3.3 fusion.95
  217.4 5.7 %scatter_fusion.1 = f32[2,24,128,64]{2,3,1,0:T(8,128)} fusion(f32[2,24,128,64]{2,3,1,0:T(8,128)} %get-tuple-element.249, s32[32]{0:T(128)S(1)} %reshape.268, f32[32,128,64]{1,2,0:T(8,128)S(1)} %bitcast.224), kind=kCustom, calls=%fused_computation.3.clone.1 | custom fusion | flops 262144 | bytes 3145984 | tf_op jit(solution)/shard_map/while/body/eval_jaxpr/vmap()/scatter-add | solution.py:62
  223.8 2.7 fusion.96
  228.4 3.1 gather_fusion
  234.0 2.5 select_reduce_fusion.2
  237.4 2.9 multiply_reduce_fusion.2
  244.9 5.4 %scatter_fusion = f32[2,24,128,64]{2,3,1,0:T(8,128)} fusion(f32[2,24,128,64]{2,3,1,0:T(8,128)} %get-tuple-element.248, s32[32]{0:T(128)S(1)} %reshape.268, f32[32,128,64]{1,2,0:T(8,128)S(1)} %bitcast.223), kind=kCustom, calls=%fused_computation.2.clone.1 | custom fusion | flops 262144 | bytes 3145984 | tf_op jit(solution)/shard_map/while/body/eval_jaxpr/vmap()/scatter-add | solution.py:62
  250.2 3.3 fusion.95
  253.5 5.5 %scatter_fusion.1 = f32[2,24,128,64]{2,3,1,0:T(8,128)} fusion(f32[2,24,128,64]{2,3,1,0:T(8,128)} %get-tuple-element.249, s32[32]{0:T(128)S(1)} %reshape.268, f32[32,128,64]{1,2,0:T(8,128)S(1)} %bitcast.224), kind=kCustom, calls=%fused_computation.3.clone.1 | custom fusion | flops 262144 | bytes 3145984 | tf_op jit(solution)/shard_map/while/body/eval_jaxpr/vmap()/scatter-add | solution.py:62
  259.7 2.7 fusion.96
  264.2 3.1 gather_fusion
  269.8 2.5 select_reduce_fusion.2
  273.2 2.9 multiply_reduce_fusion.2
  280.7 5.1 scatter_fusion
  285.8 3.3 fusion.95
  289.1 5.3 scatter_fusion.1
  295.1 2.7 fusion.96
  299.6 3.1 gather_fusion
  305.2 2.5 select_reduce_fusion.2
  308.6 2.9 multiply_reduce_fusion.2
  316.1 5.1 scatter_fusion
  321.2 3.3 fusion.95
  324.5 5.1 scatter_fusion.1
  330.3 2.7 fusion.96
  337.2 14.0 %copy.133 = bf16[4,24,128,2,64]{4,3,0,2,1:T(2,128)(2,1)} copy(bf16[4,24,128,2,64]{2,4,1,3,0:T(8,128)(2,1)} %maximum_bitcast_fusion) | data formatting | bytes 6291456 | tf_op jit(solution)/shard_map/reshape | solution.py:200
  351.2 11.9 %reshape.249 = bf16[4,3072,128]{2,0,1:T(4,128)(2,1)} reshape(bf16[4,24,128,2,64]{4,3,0,2,1:T(2,128)(2,1)} %copy.133) | data formatting | bytes 6291456 | tf_op jit(solution)/shard_map/reshape | solution.py:200
  363.1 42.1 %all_to_all.40 = bf16[4,3072,128]{2,0,1:T(4,128)(2,1)S(1)} all-to-all(bf16[4,3072,128]{2,0,1:T(4,128)(2,1)} %reshape.249), channel_id=1, replica_groups=mesh['seq_0'=4,'seq_1'=2,'batch_0'=4,'batch_1'=8] {'seq_0','seq_1'}, dimensions={1} | all-to-all | bytes 6291456 | tf_op jit(solution)/shard_map/all_to_all | solution.py:201
  408.9 4.3 fusion.39
  415.2 3.0 copy.114
  418.2 4.9 slice.42
  423.0 6.8 %copy.115 = bf16[4,2,384,1024]{3,2,1,0:T(8,128)(2,1)} copy(bf16[4,2,384,1024]{3,2,0,1:T(8,128)(2,1)} %bitcast.232) | data formatting | bytes 12582912 | tf_op jit(solution)/shard_map/transpose | solution.py:44
  429.8 32.9 %reduce-scatter.3.cloned.1.call-done = f32[256,1024]{1,0:T(8,128)} async-done(((f32[1024,1024]{1,0:T(8,128)}), f32[256,1024]{1,0:T(8,128)}) %reduce-scatter.3.cloned.1.call-update) | async-done | bytes 1048592 | tf_op jit(solution)/shard_map/reduce_scatter | solution.py:16
  462.8 6.1 %fusion.33 = bf16[1024,384]{0,1:T(8,128)(2,1)S(1)} fusion(bf16[3072,384]{0,1:T(8,128)(2,1)} %bitcast.239, bf16[3072,1024]{1,0:T(8,128)(2,1)} %bitcast.233), kind=kOutput, calls=%fused_computation.69 | convolution fusion | flops 2416312320 | bytes 9437184 | tf_op jit(solution)/shard_map/dot_general | solution.py:79
  470.1 8.3 %all-to-all-start.2 = ((bf16[32,32,384]{2,1,0:T(8,128)(2,1)}), bf16[32,32,384]{2,1,0:T(8,128)(2,1)}, u32[]{:S(2)}, u32[]{:S(2)}) async-start(bf16[32,32,384]{2,1,0:T(8,128)(2,1)} %bitcast.235), calls=%async_computation.2 | async-start | bytes 1572864 | tf_op jit(solution)/shard_map/all_to_all | solution.py:53
  490.2 18.0 %reduce-scatter.5.cloned.1.call-done = f32[32,1024]{1,0:T(8,128)} async-done(((f32[256,1024]{1,0:T(8,128)}), f32[32,1024]{1,0:T(8,128)}) %reduce-scatter.5.cloned.1.call-update) | async-done | bytes 131088 | tf_op jit(solution)/shard_map/reduce_scatter | solution.py:16
  509.8 8.0 %all-to-all-start.3 = ((f32[8,32,1,128]{3,1,2,0:T(8,128)}), f32[8,32,1,128]{3,1,2,0:T(8,128)S(1)}, u32[]{:S(2)}, u32[]{:S(2)}) async-start(f32[8,32,1,128]{3,1,2,0:T(8,128)} %bitcast.178), calls=%async_computation.5 | async-start | bytes 262144 | tf_op jit(solution)/shard_map/all_to_all | solution.py:27
  519.1 4.0 all-to-all-done.3
  (241 shorter events, 103.2 us)
Async XLA Ops:
  8.0 4.7 copy-start
  8.0 104.9 %all-gather.3.cloned.1.call-start = ((), (), s32[]{:S(2)}) async-start(), calls=%async_computation.6 | async-start | bytes 3932160 | tf_op jit(solution)/shard_map/all_gather | solution.py:40
  8.7 3.0 copy-start.11
  8.8 3.0 copy-start.16
  12.7 1.1 copy-start.13
  12.8 1.8 copy-start.15
  23.5 7.7 %copy-start.14 = (s32[1,2,24,4]{2,3,1,0:T(4,128)S(1)}, s32[1,2,24,4]{2,3,1,0:T(4,128)}, u32[]{:S(2)}) copy-start(s32[1,2,24,4]{2,3,1,0:T(4,128)} %param.11) | copy-start | bytes 2308
  23.5 66.8 %all-to-all-start = ((bf16[4,384,1024]{1,0,2:T(4,128)(2,1)}), bf16[4,384,1024]{1,0,2:T(4,128)(2,1)}, u32[]{:S(2)}, u32[]{:S(2)}) async-start(bf16[4,384,1024]{1,0,2:T(4,128)(2,1)} %copy.99), calls=%async_computation | async-start | bytes 6291456 | tf_op jit(solution)/shard_map/all_to_all | solution.py:153
  31.2 391.8 %all-gather.5.cloned.1.call-start = ((), (), s32[]{:S(2)}) async-start(), calls=%async_computation.7 | async-start | bytes 9437184 | tf_op jit(solution)/shard_map/all_gather | solution.py:40
  113.0 349.8 %reduce-scatter.3.cloned.1.call-start = ((), (), s32[]{:S(2)}) async-start(), calls=%async_computation.8 | async-start | bytes 5242880 | tf_op jit(solution)/shard_map/reduce_scatter | solution.py:16
  123.4 3.5 copy-start.3
  123.4 3.5 copy-start.5
  126.0 3.8 copy-start.4
  132.0 1.0 copy-start.2
  161.1 3.4 copy-start.3
  161.1 3.4 copy-start.5
  163.6 3.8 copy-start.4
  169.6 1.0 copy-start.2
  197.7 3.4 copy-start.3
  197.7 3.4 copy-start.5
  200.2 3.8 copy-start.4
  206.2 1.0 copy-start.2
  233.9 3.4 copy-start.3
  233.9 3.4 copy-start.5
  236.5 3.8 copy-start.4
  242.5 1.0 copy-start.2
  269.8 3.4 copy-start.3
  269.8 3.4 copy-start.5
  272.3 3.8 copy-start.4
  278.3 1.0 copy-start.2
  305.2 3.4 copy-start.3
  305.2 3.4 copy-start.5
  307.7 3.8 copy-start.4
  313.7 1.0 copy-start.2
  333.0 1.9 copy-start.1
  333.0 2.1 copy-start.9
  333.0 2.3 copy-start.10
  413.2 95.0 %reduce-scatter.5.cloned.1.call-start = ((), (), s32[]{:S(2)}) async-start(), calls=%async_computation.9 | async-start | bytes 1179648 | tf_op jit(solution)/shard_map/reduce_scatter | solution.py:16
  413.5 1.7 slice-start
  470.1 12.9 %copy-start.6 = (bf16[1,384,8,128]{3,1,2,0:T(8,128)(2,1)S(1)}, bf16[1,384,8,128]{3,1,2,0:T(8,128)(2,1)}, u32[]{:S(2)}) copy-start(bf16[1,384,8,128]{3,1,2,0:T(8,128)(2,1)} %get-tuple-element.148) | copy-start | bytes 2359300
  470.1 39.7 %all-to-all-start.2 = ((bf16[32,32,384]{2,1,0:T(8,128)(2,1)}), bf16[32,32,384]{2,1,0:T(8,128)(2,1)}, u32[]{:S(2)}, u32[]{:S(2)}) async-start(bf16[32,32,384]{2,1,0:T(8,128)(2,1)} %bitcast.235), calls=%async_computation.2 | async-start | bytes 1572864 | tf_op jit(solution)/shard_map/all_to_all | solution.py:53
  484.1 2.3 copy-start.12
  484.1 2.3 copy-start.17
  486.4 1.1 copy-start.7
  486.4 1.8 copy-start.8
  509.8 13.3 %all-to-all-start.3 = ((f32[8,32,1,128]{3,1,2,0:T(8,128)}), f32[8,32,1,128]{3,1,2,0:T(8,128)S(1)}, u32[]{:S(2)}, u32[]{:S(2)}) async-start(f32[8,32,1,128]{3,1,2,0:T(8,128)} %bitcast.178), calls=%async_computation.5 | async-start | bytes 262144 | tf_op jit(solution)/shard_map/all_to_all | solution.py:27
Sparse Core Ops, SparseCore 0:
  10.6 70.1 all-gather.2
  113.1 22.5 all-gather.4
Sparse Core Ops, SparseCore 1:
  413.3 49.4 reduce-scatter.2
  465.2 43.0 reduce-scatter.4
where the time goes:
time: 539 us; the launch traced here: 531 us
  local copies, waits for them, and re-layouts  137 us (25%)
  waiting for transfers between devices  115 us (21%)
  matrix products  111 us (21%)
  other arithmetic  85.1 us (16%)
  blocking collectives  42.1 us (8%)
  starting transfers between devices  24.5 us (5%)
  between operations  15.7 us (3%)
    scatter-add x18, other arithmetic, add_blocks(): return running.at[chosen].add(portion)  67.1 us
    all_to_all x1, waiting for transfers between devices, per_device(): lax.all_to_all(stacked, SEQ, split_axis=2, concat_axis=1, tiled=True)  59 us
    reduce_scatter x2, waiting for transfers between devices, sum_by_axis(): subtotal = lax.psum_scatter(subtotal, axis, scatter_dimension=0, tiled=True)  50.9 us
    all_to_all x1, blocking collectives, per_device(): lax.all_to_all(head_grads, SEQ, split_axis=1, concat_axis=2, tiled=True)  42.1 us
    gather x18, local copies, waits for them, and re-layouts, pick_blocks(): return source[chosen]  32 us
    reshape x2, local copies, waits for them, and re-layouts, per_device(): head_grads.transpose(0, 2, 3, 1, 4).reshape(4, seq_len, head_width)  25.9 us
    dot_general x6, matrix products, attend_group(): jnp.einsum('hgqnk,hgqd->hgnkd', probs_half, out_grads, preferred_element_...  19.7 us
    dot_general x6, matrix products, attend_group(): jnp.einsum('hgqnk,hgnkd->hgqd', probs_half, picked_values, preferred_elem...  17.5 us
  transfers between devices with their start and end apart: 7, of which 4 were waited for; matrix products, arithmetic and copies ran while one was open for 61% of the time, Pallas kernels for 0%

commit v1 on v0

v1 whole, which is shorter than its diff:
```python
import functools
import math

import jax
import jax.numpy as jnp
from jax import lax
from jax.experimental import pallas as pl
from jax.experimental.pallas import tpu as pltpu
from jax.sharding import Mesh
from jax.sharding import PartitionSpec as P


BLK = 128
HEADS = 2
HD = 64
NT = (((1,), (1,)), ((), ()))


def dot(a, b):
    return jnp.dot(a, b, preferred_element_type=jnp.float32)


def dot_nt(a, b):
    return lax.dot_general(a, b, NT, preferred_element_type=jnp.float32)


def attend_head(head, block, listed, q, k, v, do, kt, vt, dot_, key_acc, value_acc, flipped):
    lanes = lax.broadcasted_iota(jnp.int32, (BLK, BLK), 1)
    mine = (lanes >= HD) if head else (lanes < HD)
    rows = pl.ds(head * HD, HD)
    own = pl.ds(pl.multiple_of(block * BLK, BLK), BLK)
    starts = [pl.ds(pl.multiple_of(n * BLK, BLK), BLK) for n in listed]
    query = jnp.where(mine, q[own, :], jnp.zeros((), jnp.bfloat16))
    grad = jnp.where(mine, do[own, :], jnp.zeros((), jnp.bfloat16))
    scores = [dot_nt(k[s, :], query) for s in starts]
    key_at = lax.broadcasted_iota(jnp.int32, (BLK, BLK), 0)
    scores[0] = jnp.where(key_at <= lanes, scores[0], -jnp.inf)
    prob_grad = [dot_nt(v[s, :], grad) for s in starts]
    top = scores[0]
    for s in scores[1:]:
        top = jnp.maximum(top, s)
    top = jnp.max(top, axis=0, keepdims=True)
    raised = [jnp.exp((s - top) * (1.0 / 8.0)) for s in scores]
    total = raised[0]
    for e in raised[1:]:
        total = total + e
    share = 1.0 / jnp.sum(total, axis=0, keepdims=True)
    probs = [e * share for e in raised]
    halves = [p.astype(jnp.bfloat16) for p in probs]
    stacked = jnp.concatenate(halves, axis=0)
    attended = dot(jnp.concatenate([vt[n, rows, :] for n in listed], axis=1), stacked)
    attended = attended.astype(jnp.bfloat16)
    delta = jnp.sum(
        dot_[block, rows, :].astype(jnp.float32) * attended.astype(jnp.float32), axis=0, keepdims=True
    )
    score_grads = [
        (p * (g - delta)).astype(jnp.bfloat16) for p, g in zip(probs, prob_grad)
    ]
    graded = jnp.concatenate(score_grads, axis=0)
    query_grad = dot(jnp.concatenate([kt[n, rows, :] for n in listed], axis=1), graded)
    flipped[0, block, rows, :] = (query_grad * (1.0 / 8.0)).astype(jnp.bfloat16)
    flipped[3, block, rows, :] = attended
    value_part = dot(stacked, grad)
    key_part = dot(graded, query)
    for i, s in enumerate(starts):
        value_acc[s, :] += value_part[i * BLK : (i + 1) * BLK]
        key_acc[s, :] += key_part[i * BLK : (i + 1) * BLK]


def attention_kernel(offs, heads, turned, grads, flipped, key_acc, value_acc):
    q, k, v, do = (heads.at[n] for n in range(4))
    kt, vt, dot_ = (turned.at[n] for n in range(3))
    blocks = heads.shape[1] // BLK
    key_acc[...] = jnp.zeros_like(key_acc)
    value_acc[...] = jnp.zeros_like(value_acc)

    @pl.loop(0, blocks)
    def _(block):
        for head in range(HEADS):
            o1 = offs[head, block * 4 + 1]
            o2 = offs[head, block * 4 + 2]
            o3 = offs[head, block * 4 + 3]
            v1 = (o1 <= block).astype(jnp.int32)
            v2 = (o2 <= block).astype(jnp.int32)
            v3 = (o3 <= block).astype(jnp.int32)
            count = v1 + v2 + v3
            first = jnp.where(v1 == 1, o1, jnp.where(v2 == 1, o2, o3))
            second = jnp.where(v1 + v2 == 2, o2, o3)
            for extra in range(4):
                picked = [block] + [
                    jnp.maximum(block - o, 0) for o in (first, second, o3)[:extra]
                ]

                @pl.when(count == extra)
                def _(picked=picked, head=head):
                    attend_head(
                        head, block, picked, q, k, v, do, kt, vt, dot_, key_acc, value_acc, flipped
                    )

    @pl.loop(0, blocks)
    def _(block):
        own = pl.ds(pl.multiple_of(block * BLK, BLK), BLK)
        grads[0, own, :] = flipped[0, block].T
        kg = (key_acc[own, :] * (1.0 / 8.0)).astype(jnp.bfloat16)
        vg = value_acc[own, :].astype(jnp.bfloat16)
        grads[1, own, :] = kg
        grads[2, own, :] = vg
        flipped[1, block] = kg.T
        flipped[2, block] = vg.T


def attention(offsets, heads, turned):
    length, width = heads.shape[1:]
    blocks = length // BLK
    whole = pl.BlockSpec(memory_space=pltpu.VMEM)
    return pl.pallas_call(
        attention_kernel,
        out_shape=(
            jax.ShapeDtypeStruct((3, length, width), jnp.bfloat16),
            jax.ShapeDtypeStruct((4, blocks, width, BLK), jnp.bfloat16),
        ),
        in_specs=[pl.BlockSpec(memory_space=pltpu.SMEM)] + [whole] * 2,
        out_specs=(whole, whole),
        scratch_shapes=[
            pltpu.VMEM((length, width), jnp.float32),
            pltpu.VMEM((length, width), jnp.float32),
        ],
        compiler_params=pltpu.CompilerParams(vmem_limit_bytes=48 << 20),
        cost_estimate=pl.CostEstimate(flops=4 << 30, bytes_accessed=12 << 20, transcendentals=3 << 20),
        name="attention",
    )(offsets.reshape(HEADS, -1), heads, turned)


ROWS = 384
HALF = 192
WIDTH = 128
D = 1024
CHUNKS = 8


def remote(src, dst, send, recv, **where):
    return pltpu.make_async_remote_copy(
        src_ref=src, dst_ref=dst, send_sem=send, recv_sem=recv,
        device_id=where, device_id_type=pl.DeviceIdType.MESH,
    )


def gather_kernel(
    hidden, grad_out, w_query, w_key, w_value, w_out, rows_all, heads, flipped,
    land, w_in, w_back, heads_v, flipped_v, send, recv, load, save,
):
    y, c = lax.axis_index("seq_0"), lax.axis_index("seq_1")
    right, left, opposite = (y + 1) % 4, (y + 3) % 4, (y + 2) % 4
    own = 2 * y + c
    to_right = dict(seq_0=right, seq_1=c)
    to_left = dict(seq_0=left, seq_1=c)
    to_mate = dict(seq_0=y, seq_1=1 - c)
    upper, lower = pl.ds(0, HALF), pl.ds(HALF, HALF)
    both = pl.ds(0, ROWS)
    sources = (hidden, grad_out)

    barrier = pltpu.get_barrier_semaphore()
    for peer in (to_right, to_left, to_mate):
        pl.semaphore_signal(barrier, inc=1, device_id=peer, device_id_type=pl.DeviceIdType.MESH)
    pl.semaphore_wait(barrier, 3)

    def place(a, chunk, part):
        return land.at[a, chunk, part]

    def copy(a, slot, chunk, part, where, src=None):
        at = place(a, chunk, part)
        return remote(at if src is None else src, at, send.at[a, slot], recv.at[a, slot], **where)

    def arrived(a, slot, chunk, part):
        copy(a, slot, chunk, part, to_mate).wait_recv()

    def start_own(a):
        src = sources[a]
        copy(a, 0, own, upper, to_right, src.at[upper]).start()
        copy(a, 3, own, lower, to_left, src.at[lower]).start()
        copy(a, 1, own, lower, to_right, src.at[lower]).start()
        copy(a, 4, own, upper, to_left, src.at[upper]).start()
        copy(a, 6, own, both, to_mate, src).start()

    def relay_near(a):
        arrived(a, 0, 2 * left + c, upper)
        copy(a, 2, 2 * left + c, upper, to_right).start()
        copy(a, 7, 2 * left + c, upper, to_mate).start()
        arrived(a, 3, 2 * right + c, lower)
        copy(a, 5, 2 * right + c, lower, to_left).start()
        copy(a, 9, 2 * right + c, lower, to_mate).start()

    def relay_rest(a):
        arrived(a, 1, 2 * left + c, lower)
        copy(a, 8, 2 * left + c, lower, to_mate).start()
        arrived(a, 4, 2 * right + c, upper)
        copy(a, 10, 2 * right + c, upper, to_mate).start()

    def relay_far(a):
        arrived(a, 2, 2 * opposite + c, upper)
        copy(a, 11, 2 * opposite + c, upper, to_mate).start()
        arrived(a, 5, 2 * opposite + c, lower)
        copy(a, 12, 2 * opposite + c, lower, to_mate).start()

    def project(a, count, chip_of):
        @pl.loop(0, count)
        def _(j):
            chunk = 2 * chip_of(j // 2) + j % 2
            pltpu.make_async_copy(land.at[a, chunk], rows_all.at[a, chunk], save.at[a]).start()
            at = pl.ds(pl.multiple_of(chunk * ROWS, ROWS), ROWS)
            x = land[a, chunk]
            if a == 0:
                for n in range(3):
                    part = dot(x, w_in[n]).astype(jnp.bfloat16)
                    heads_v[n, at, :] = part
                    if n > 0:
                        for i in range(3):
                            flipped_v[n - 1, chunk * 3 + i] = part[i * BLK : (i + 1) * BLK].T
            else:
                part = dot_nt(x, w_back[...]).astype(jnp.bfloat16)
                heads_v[3, at, :] = part
                for i in range(3):
                    flipped_v[2, chunk * 3 + i] = part[i * BLK : (i + 1) * BLK].T

    mine = pl.ds(pl.multiple_of(own * WIDTH, WIDTH), WIDTH)
    start_own(0)
    loads = [
        pltpu.make_async_copy(hidden, land.at[0, own], load.at[0]),
        pltpu.make_async_copy(w_query.at[:, mine], w_in.at[0], load.at[1]),
        pltpu.make_async_copy(w_key.at[:, mine], w_in.at[1], load.at[2]),
        pltpu.make_async_copy(w_value.at[:, mine], w_in.at[2], load.at[3]),
        pltpu.make_async_copy(grad_out, land.at[1, own], load.at[4]),
        pltpu.make_async_copy(w_out.at[mine, :], w_back, load.at[5]),
    ]
    for item in loads:
        item.start()
    relay_near(0)
    start_own(1)
    for item in loads:
        item.wait()
    for a in range(2):
        if a == 1:
            relay_near(1)
        arrived(a, 6, 2 * y + 1 - c, both)
        project(a, 2, lambda i: y)
        relay_rest(a)
        arrived(a, 7, 2 * left + 1 - c, upper)
        arrived(a, 9, 2 * right + 1 - c, lower)
        arrived(a, 8, 2 * left + 1 - c, lower)
        arrived(a, 10, 2 * right + 1 - c, upper)
        project(a, 4, lambda i: (y + 1 + 2 * i) % 4)
        relay_far(a)
        arrived(a, 11, 2 * opposite + 1 - c, upper)
        arrived(a, 12, 2 * opposite + 1 - c, lower)
        project(a, 2, lambda i: opposite)
        first = 0 if a == 0 else 3
        count = 3 if a == 0 else 1
        pltpu.make_async_copy(
            heads_v.at[pl.ds(first, count)], heads.at[pl.ds(first, count)], save.at[2 + a]
        ).start()
        first, count = (0, 2) if a == 0 else (2, 1)
        pltpu.make_async_copy(
            flipped_v.at[pl.ds(first, count)], flipped.at[pl.ds(first, count)], save.at[4 + a]
        ).start()
    for a in range(2):
        pltpu.make_async_copy(land.at[a], rows_all.at[a], save.at[a]).wait()
        first, count = (0, 3) if a == 0 else (3, 1)
        pltpu.make_async_copy(
            heads_v.at[pl.ds(first, count)], heads.at[pl.ds(first, count)], save.at[2 + a]
        ).wait()
        first, count = (0, 2) if a == 0 else (2, 1)
        pltpu.make_async_copy(
            flipped_v.at[pl.ds(first, count)], flipped.at[pl.ds(first, count)], save.at[4 + a]
        ).wait()
        for slot, chunk, part in (
            (0, own, upper), (1, own, lower), (2, 2 * left + c, upper),
            (3, own, lower), (4, own, upper), (5, 2 * right + c, lower),
            (6, own, both), (7, 2 * left + c, upper), (8, 2 * left + c, lower),
            (9, 2 * right + c, lower), (10, 2 * right + c, upper),
            (11, 2 * opposite + c, upper), (12, 2 * opposite + c, lower),
        ):
            copy(a, slot, chunk, part, to_mate).wait_send()


def gather(hidden, grad_out, w_query, w_key, w_value, w_out):
    anywhere = pl.BlockSpec(memory_space=pl.ANY)
    length = CHUNKS * ROWS
    blocks = length // BLK
    bf16 = jnp.bfloat16
    return pl.pallas_call(
        gather_kernel,
        out_shape=(
            jax.ShapeDtypeStruct((2, CHUNKS, ROWS, D), bf16),
            jax.ShapeDtypeStruct((4, length, WIDTH), bf16),
            jax.ShapeDtypeStruct((3, blocks, BLK, BLK), bf16),
        ),
        in_specs=[anywhere] * 6,
        out_specs=(anywhere,) * 3,
        scratch_shapes=[
            pltpu.VMEM((2, CHUNKS, ROWS, D), bf16),
            pltpu.VMEM((3, D, WIDTH), bf16),
            pltpu.VMEM((WIDTH, D), bf16),
            pltpu.VMEM((4, length, WIDTH), bf16),
            pltpu.VMEM((3, blocks, BLK, BLK), bf16),
            pltpu.SemaphoreType.DMA((2, 13)),
            pltpu.SemaphoreType.DMA((2, 13)),
            pltpu.SemaphoreType.DMA((6,)),
            pltpu.SemaphoreType.DMA((6,)),
        ],
        compiler_params=pltpu.CompilerParams(
            collective_id=0, has_side_effects=True, vmem_limit_bytes=60 << 20
        ),
        name="gather_and_project",
    )(hidden, grad_out, w_query, w_key, w_value, w_out)


SHIFTS = ((0, 1), (1, 0), (1, 1), (3, 0), (3, 1), (2, 0), (2, 1))


def return_kernel(
    norm, rows_all, grads, flipped, w_query, w_key, w_value, grad_hidden, grad_weights,
    rows_v, flipped_v, w_v, back, out_acc, back_part, part_acc, part, x_in, z_out, z_in,
    y_send, y_recv, o_send, o_recv, x_send, x_recv, z_send, z_recv, load,
):
    y, c = lax.axis_index("seq_0"), lax.axis_index("seq_1")
    x, z = lax.axis_index("batch_0"), lax.axis_index("batch_1")
    own = 2 * y + c
    peers = [dict(seq_0=(y + dy) % 4, seq_1=(c + dc) % 2) for dy, dc in SHIFTS]
    x_peers = [(x + i) % 4 for i in (1, 3, 2)]
    z_peers = [(z + i) % 8 for i in (1, 7, 2, 6, 3, 5, 4)]

    barrier = pltpu.get_barrier_semaphore()
    everyone = peers + [dict(batch_0=p) for p in x_peers] + [dict(batch_1=p) for p in z_peers]
    for peer in everyone:
        pl.semaphore_signal(barrier, inc=1, device_id=peer, device_id_type=pl.DeviceIdType.MESH)
    pl.semaphore_wait(barrier, len(everyone))

    def chunk_of(peer):
        return 2 * peer["seq_0"] + peer["seq_1"]

    def lanes(chunk):
        return pl.ds(pl.multiple_of(chunk * WIDTH, WIDTH), WIDTH)

    def rows(chunk):
        return pl.ds(pl.multiple_of(chunk * ROWS, ROWS), ROWS)

    def y_copy(a, i):
        peer = peers[i]
        return remote(
            grads.at[a, rows(chunk_of(peer))], back.at[a, :, lanes(own)],
            y_send.at[a, i], y_recv.at[a, own], **peer,
        )

    def y_wait(a, chunk):
        pltpu.make_async_remote_copy(
            src_ref=grads.at[a, rows(chunk)], dst_ref=back.at[a, :, lanes(chunk)],
            send_sem=y_send.at[a, 0], recv_sem=y_recv.at[a, chunk],
            device_id=peers[0], device_id_type=pl.DeviceIdType.MESH,
        ).wait_recv()

    loads = [
        pltpu.make_async_copy(rows_all.at[1], rows_v.at[1], load.at[0]),
        pltpu.make_async_copy(flipped, flipped_v, load.at[1]),
        pltpu.make_async_copy(rows_all.at[0], rows_v.at[0], load.at[2]),
        pltpu.make_async_copy(w_query, w_v.at[0], load.at[3]),
        pltpu.make_async_copy(w_key, w_v.at[1], load.at[4]),
        pltpu.make_async_copy(w_value, w_v.at[2], load.at[5]),
    ] + [
        pltpu.make_async_copy(grads.at[a, rows(own)], back.at[a, :, lanes(own)], load.at[6 + a])
        for a in range(3)
    ]
    for item in loads[:2]:
        item.start()
    for i in range(7):
        y_copy(2, i).start()
    for item in loads[2:]:
        item.start()

    def side_by_side(a, j):
        return jnp.concatenate([flipped_v[a, 3 * j + i] for i in range(3)], axis=1)

    loads[0].wait()
    loads[1].wait()
    part_acc[0:WIDTH] = dot(side_by_side(3, 0), rows_v[1, 0])

    @pl.loop(1, CHUNKS)
    def _(j):
        part_acc[0:WIDTH] += dot(side_by_side(3, j), rows_v[1, j])

    back_part[...] = part_acc[0:WIDTH].astype(jnp.bfloat16)

    def o_copy(i):
        peer = peers[i]
        return remote(
            back_part.at[:, lanes(chunk_of(peer))], part.at[3, lanes(own)],
            o_send.at[i], o_recv.at[own], **peer,
        )

    def o_wait(chunk):
        pltpu.make_async_remote_copy(
            src_ref=back_part.at[:, lanes(chunk)], dst_ref=part.at[3, lanes(chunk)],
            send_sem=o_send.at[0], recv_sem=o_recv.at[chunk],
            device_id=peers[0], device_id_type=pl.DeviceIdType.MESH,
        ).wait_recv()

    for i in range(7):
        o_copy(i).start()
    for a in (1, 0):
        for i in range(7):
            y_copy(a, i).start()
    part[3, lanes(own), :] = back_part[:, lanes(own)]

    loads[2].wait()

    def three(j):
        return jnp.concatenate([side_by_side(a, j) for a in range(3)], axis=0)

    part_acc[...] = dot(three(0), rows_v[0, 0])

    @pl.loop(1, CHUNKS)
    def _(j):
        part_acc[...] += dot(three(j), rows_v[0, j])

    @pl.loop(0, 8)
    def _(t):
        for a in range(3):
            tile = part_acc[pl.ds(a * WIDTH, WIDTH), lanes(t)]
            part[a, lanes(t), :] = tile.T.astype(jnp.bfloat16)

    quarter = D // 4

    def x_copy(k, i):
        p = x_peers[i]
        which = pl.ds(0, 3) if k == 0 else pl.ds(3, 1)
        return remote(
            part.at[which, pl.ds(pl.multiple_of(p * quarter, quarter), quarter)],
            x_in.at[x, which], x_send.at[k, i], x_recv.at[k, x], batch_0=p,
        )

    def x_wait(k, p):
        which = pl.ds(0, 3) if k == 0 else pl.ds(3, 1)
        pltpu.make_async_remote_copy(
            src_ref=x_in.at[p, which], dst_ref=x_in.at[p, which],
            send_sem=x_send.at[k, 0], recv_sem=x_recv.at[k, p],
            device_id=dict(batch_0=x_peers[0]), device_id_type=pl.DeviceIdType.MESH,
        ).wait_recv()

    for i in range(3):
        x_copy(0, i).start()
    for item in loads[3:]:
        item.wait()

    def add_chips(count, chip_of, first):
        @pl.loop(0, count)
        def _(j):
            at = pl.ds(pl.multiple_of(chip_of(j) * 2 * WIDTH, 2 * WIDTH), 2 * WIDTH)
            total = dot_nt(back[0, :, at], w_v[0, :, at])
            total += dot_nt(back[1, :, at], w_v[1, :, at])
            total += dot_nt(back[2, :, at], w_v[2, :, at])
            if first:
                out_acc[...] = total
            else:
                out_acc[...] += total

    for a in (2, 1, 0):
        y_wait(a, 2 * y + 1 - c)
    add_chips(1, lambda j: y, True)

    for peer in peers:
        o_wait(chunk_of(peer))
    for i in range(3):
        x_copy(1, i).start()
    for p in x_peers:
        x_wait(0, p)
    for p in x_peers:
        x_wait(1, p)
    total = part[:, pl.ds(pl.multiple_of(x * quarter, quarter), quarter), :].astype(jnp.float32)
    for p in x_peers:
        total += x_in[p].astype(jnp.float32)
    z_out[...] = total.astype(jnp.bfloat16)

    def z_copy(i):
        p = z_peers[i]
        return remote(
            z_out.at[:, pl.ds(pl.multiple_of(p * 32, 32), 32)], z_in.at[z],
            z_send.at[i], z_recv.at[z], batch_1=p,
        )

    def z_wait(p):
        pltpu.make_async_remote_copy(
            src_ref=z_in.at[p], dst_ref=z_in.at[p],
            send_sem=z_send.at[0], recv_sem=z_recv.at[p],
            device_id=dict(batch_1=z_peers[0]), device_id_type=pl.DeviceIdType.MESH,
        ).wait_recv()

    for i in range(7):
        z_copy(i).start()

    for a in (2, 1, 0):
        for peer in peers[1:5]:
            y_wait(a, chunk_of(peer))
    add_chips(2, lambda j: (y + 1 + 2 * j) % 4, False)

    for p in z_peers:
        z_wait(p)
    total = z_out[:, pl.ds(pl.multiple_of(z * 32, 32), 32), :].astype(jnp.float32)
    for p in z_peers:
        total += z_in[p].astype(jnp.float32)
    grad_weights[...] = total * norm

    for a in (2, 1, 0):
        for peer in peers[5:]:
            y_wait(a, chunk_of(peer))
    at = pl.ds(pl.multiple_of(((y + 2) % 4) * 2 * WIDTH, 2 * WIDTH), 2 * WIDTH)
    total = dot_nt(back[0, :, at], w_v[0, :, at])
    total += dot_nt(back[1, :, at], w_v[1, :, at])
    total += dot_nt(back[2, :, at], w_v[2, :, at])
    grad_hidden[...] = (out_acc[...] + total).astype(jnp.bfloat16)

    for i in range(7):
        for a in range(3):
            y_copy(a, i).wait_send()
        o_copy(i).wait_send()
        z_copy(i).wait_send()
    for i in range(3):
        for k in range(2):
            x_copy(k, i).wait_send()


def hand_back(rows_all, grads, flipped, w_query, w_key, w_value, norm):
    anywhere = pl.BlockSpec(memory_space=pl.ANY)
    whole = pl.BlockSpec(memory_space=pltpu.VMEM)
    bf16 = jnp.bfloat16
    f32 = jnp.float32
    blocks = CHUNKS * ROWS // BLK
    dma = pltpu.SemaphoreType.DMA
    return pl.pallas_call(
        functools.partial(return_kernel, norm),
        out_shape=(
            jax.ShapeDtypeStruct((ROWS, D), bf16),
            jax.ShapeDtypeStruct((4, 32, WIDTH), f32),
        ),
        in_specs=[anywhere] * 6,
        out_specs=(whole, whole),
        scratch_shapes=[
            pltpu.VMEM((2, CHUNKS, ROWS, D), bf16),
            pltpu.VMEM((4, blocks, BLK, BLK), bf16),
            pltpu.VMEM((3, D, D), bf16),
            pltpu.VMEM((3, ROWS, D), bf16),
            pltpu.VMEM((ROWS, D), f32),
            pltpu.VMEM((WIDTH, D), bf16),
            pltpu.VMEM((3 * WIDTH, D), f32),
            pltpu.VMEM((4, D, WIDTH), bf16),
            pltpu.VMEM((4, 4, D // 4, WIDTH), bf16),
            pltpu.VMEM((4, D // 4, WIDTH), bf16),
            pltpu.VMEM((8, 4, 32, WIDTH), bf16),
            dma((3, 7)), dma((3, 8)), dma((7,)), dma((8,)),
            dma((2, 3)), dma((2, 4)), dma((7,)), dma((8,)), dma((9,)),
        ],
        compiler_params=pltpu.CompilerParams(
            collective_id=1, has_side_effects=True, vmem_limit_bytes=60 << 20
        ),
        name="return_and_reduce",
    )(rows_all, grads, flipped, w_query, w_key, w_value)


BATCH = ("batch_0", "batch_1")
SEQ = ("seq_0", "seq_1")


def per_device(hidden, grad_out, block_offsets, w_query, w_key, w_value, w_out):
    norm = 1.0 / math.sqrt(ROWS * lax.axis_size(SEQ) * lax.axis_size(BATCH))
    rows_all, heads, turned = gather(hidden[0], grad_out[0], w_query, w_key, w_value, w_out)
    grads, flipped = attention(block_offsets[0], heads, turned)
    grad_hidden, grad_weights = hand_back(
        rows_all, grads, flipped, w_query, w_key, w_value, norm
    )
    return (grad_hidden[None], grad_weights)


def solution(mesh):
    torus = Mesh(mesh.devices.reshape(4, 2, 4, 8), ("seq_0", "seq_1", "batch_0", "batch_1"))
    in_specs = (
        P(BATCH, SEQ, None),
        P(BATCH, SEQ, None),
        P(BATCH, SEQ, None, None),
        P(),
        P(),
        P(),
        P(),
    )
    out_specs = (P(BATCH, SEQ, None), P(None, BATCH, SEQ))
    return jax.shard_map(
        per_device, mesh=torus, in_specs=in_specs, out_specs=out_specs, check_vma=False
    )
```

time: 539 us -> 150 us (0.28); the launches traced: 531 us -> 149 us
  Pallas kernels: 0 us -> 141 us
  local copies, waits for them, and re-layouts: 137 us -> 7.46 us
  waiting for transfers between devices: 115 us -> 0 us
  matrix products: 111 us -> 0 us
  other arithmetic: 85.1 us -> 0 us
  blocking collectives: 42.1 us -> 0 us
  starting transfers between devices: 24.5 us -> 0 us
  between operations: 15.7 us -> 0.66 us
    pallas_call x0 -> x3, Pallas kernels: none -> 141 us  [the longest x1 61.1 us: gather(): pl.pallas_call(gather_kernel, out_shape=(jax.ShapeDtypeStruct((2, CHUNKS,...]
    dot_general x45 -> x0, matrix products: 111 us -> none  [the longest x6 19.7 us: attend_group(): jnp.einsum('hgqnk,hgqd->hgnkd', probs_half, out_grads, preferred_element_...]
    scatter-add x18 -> x0, other arithmetic: 67.1 us -> none  [add_blocks(): return running.at[chosen].add(portion)]
    all_to_all x3 -> x0, waiting for transfers between devices: 63 us -> none  [the longest x1 59 us: per_device(): lax.all_to_all(stacked, SEQ, split_axis=2, concat_axis=1, tiled=True)]
    reduce_scatter x2 -> x0, waiting for transfers between devices: 50.9 us -> none  [sum_by_axis(): subtotal = lax.psum_scatter(subtotal, axis, scatter_dimension=0, tiled=True)]
    all_to_all x1 -> x0, blocking collectives: 42.1 us -> none  [per_device(): lax.all_to_all(head_grads, SEQ, split_axis=1, concat_axis=2, tiled=True)]
    gather x18 -> x0, local copies, waits for them, and re-layouts: 32 us -> none  [pick_blocks(): return source[chosen]]
    reshape x4 -> x0, local copies, waits for them, and re-layouts: 31.8 us -> none  [the longest x2 25.9 us: per_device(): head_grads.transpose(0, 2, 3, 1, 4).reshape(4, seq_len, head_width)]
  transfers between devices with their start and end apart: 7 -> 0, of which waited for: 4 -> 0; matrix products, arithmetic and copies ran while one was open for 61% -> 0% of each run, Pallas kernels for 0% -> 0%
where the time goes in v1:
time: 150 us; the launch traced here: 149 us
  Pallas kernels  141 us (94%)
  local copies, waits for them, and re-layouts  7.46 us (5%)
    pallas_call x1, Pallas kernels, gather(): pl.pallas_call(gather_kernel, out_shape=(jax.ShapeDtypeStruct((2, CHUNKS,...  61.1 us
    pallas_call x1, Pallas kernels, hand_back(): pl.pallas_call(functools.partial(return_kernel, norm), out_shape=(jax.Sha...  41.9 us
    pallas_call x1, Pallas kernels, attention(): pl.pallas_call(attention_kernel, out_shape=(jax.ShapeDtypeStruct((3, leng...  38.2 us
    unnamed x7, local copies, waits for them, and re-layouts  7.36 us

profile of v1, /device:TPU:1, one launch (start us, length us, event | category | flops | bytes accessed | tf_op | source)
XLA Modules:
  0.0 149.3 jit_solution(8370369292367660375)
XLA Ops:
  0.6 0.8 copy.10
  1.4 0.1 reshape_squeeze.3.offs
  1.5 61.1 %gather_and_project.1 = (bf16[2,8,384,1024]{3,2,1,0:T(8,128)(2,1)}, bf16[4,3072,128]{2,1,0:T(8,128)(2,1)}, bf16[3,24,128,128]{3,2,1,0:T(8,128)(2,1)}) custom-call(bf16[384,1024]{1,0:T(8,128)(2,1)} %bitcast.5, bf16[384,1024]{1,0:T(8,128)(2,1)} %bitcast.6, bf16[1024,1024]{1,0:T(8,128)(2,1)} %w_query.3, bf16[1024,1024]{1,0:T(8,128)(2,1)} %w_key.3, ...), custom_call_target="tpu_custom_call" | custom-call | tf_op jit(solution)/shard_map/gather_and_project/pallas_call | solution.py:290
  62.6 0.0 copy-start.1
  62.6 1.7 %copy-done.1 = bf16[3,24,128,128]{3,2,1,0:T(8,128)(2,1)S(1)} copy-done((bf16[3,24,128,128]{3,2,1,0:T(8,128)(2,1)S(1)}, bf16[3,24,128,128]{3,2,1,0:T(8,128)(2,1)}, u32[]{:S(2)}) %copy-start.1) | copy-done | bytes 2359320
  64.3 38.2 %attention.1 = (bf16[3,3072,128]{2,1,0:T(8,128)(2,1)S(1)}, bf16[4,24,128,128]{3,2,1,0:T(8,128)(2,1)}) custom-call(s32[2,96]{1,0:T(2,128)S(1)} %reshape_squeeze.3.offs, bf16[4,3072,128]{2,1,0:T(8,128)(2,1)} %get-tuple-element.10.heads, bf16[3,24,128,128]{3,2,1,0:T(8,128)(2,1)S(1)} %copy-done.1), custom_call_target="tpu_custom_call" | custom-call | flops 4294967296 | bytes 12582912 | tf_op jit(solution)/shard_map/attention/pallas_call | solution.py:116
  102.5 0.0 copy-start
  102.5 1.4 copy-done
  103.9 41.9 %return_and_reduce.1 = (bf16[384,1024]{1,0:T(8,128)(2,1)}, f32[4,32,128]{2,1,0:T(8,128)}) custom-call(bf16[2,8,384,1024]{3,2,1,0:T(8,128)(2,1)} %get-tuple-element.9.rows_all, bf16[3,3072,128]{2,1,0:T(8,128)(2,1)} %copy-done, bf16[4,24,128,128]{3,2,1,0:T(8,128)(2,1)} %get-tuple-element.13.flipped, bf16[1024,1024]{1,0:T(8,128)(2,1)} %w_query.3, ...), custom_call_target="tpu_custom_call" | custom-call | tf_op jit(solution)/shard_map/return_and_reduce/pallas_call | solution.py:537
  145.8 2.1 %copy.13 = bf16[1,384,1024]{2,1,0:T(8,128)(2,1)} copy(bf16[1,384,1024]{2,1,0:T(8,128)(2,1)} %bitcast.7) | data formatting | bytes 1572864
  147.9 1.5 copy.14
Async XLA Ops:
  62.6 1.7 %copy-start.1 = (bf16[3,24,128,128]{3,2,1,0:T(8,128)(2,1)S(1)}, bf16[3,24,128,128]{3,2,1,0:T(8,128)(2,1)}, u32[]{:S(2)}) copy-start(bf16[3,24,128,128]{3,2,1,0:T(8,128)(2,1)} %get-tuple-element.11.turned) | copy-start | bytes 7077892
  102.5 1.4 copy-start

commit v2 on v1

--- a/solution.py
+++ b/solution.py
@@ -13,6 +13,8 @@
 BLK = 128
 HEADS = 2
 HD = 64
+GROUP = 3
+PIECES = 4
 NT = (((1,), (1,)), ((), ()))
 
 
@@ -24,108 +26,206 @@
     return lax.dot_general(a, b, NT, preferred_element_type=jnp.float32)
 
 
-def attend_head(head, block, listed, q, k, v, do, kt, vt, dot_, key_acc, value_acc, flipped):
+def rows_of(block):
+    return pl.ds(pl.multiple_of(block * BLK, BLK), BLK)
+
+
+def slots_of(offs, head, block):
+    o1, o2, o3 = (offs[head, block * 4 + i] for i in (1, 2, 3))
+    v1, v2, v3 = ((o <= block).astype(jnp.int32) for o in (o1, o2, o3))
+    first = jnp.where(v1 == 1, o1, jnp.where(v2 == 1, o2, o3))
+    second = jnp.where(v1 + v2 == 2, o2, o3)
+    return v1 + v2 + v3, (first, second, o3)
+
+
+def attend(jobs, width, blocks, q, k, v, do, kt, vt, acc, flipped):
     lanes = lax.broadcasted_iota(jnp.int32, (BLK, BLK), 1)
-    mine = (lanes >= HD) if head else (lanes < HD)
-    rows = pl.ds(head * HD, HD)
-    own = pl.ds(pl.multiple_of(block * BLK, BLK), BLK)
-    starts = [pl.ds(pl.multiple_of(n * BLK, BLK), BLK) for n in listed]
-    query = jnp.where(mine, q[own, :], jnp.zeros((), jnp.bfloat16))
-    grad = jnp.where(mine, do[own, :], jnp.zeros((), jnp.bfloat16))
-    scores = [dot_nt(k[s, :], query) for s in starts]
     key_at = lax.broadcasted_iota(jnp.int32, (BLK, BLK), 0)
-    scores[0] = jnp.where(key_at <= lanes, scores[0], -jnp.inf)
-    prob_grad = [dot_nt(v[s, :], grad) for s in starts]
-    top = scores[0]
-    for s in scores[1:]:
-        top = jnp.maximum(top, s)
-    top = jnp.max(top, axis=0, keepdims=True)
-    raised = [jnp.exp((s - top) * (1.0 / 8.0)) for s in scores]
-    total = raised[0]
-    for e in raised[1:]:
-        total = total + e
-    share = 1.0 / jnp.sum(total, axis=0, keepdims=True)
-    probs = [e * share for e in raised]
-    halves = [p.astype(jnp.bfloat16) for p in probs]
-    stacked = jnp.concatenate(halves, axis=0)
-    attended = dot(jnp.concatenate([vt[n, rows, :] for n in listed], axis=1), stacked)
-    attended = attended.astype(jnp.bfloat16)
-    delta = jnp.sum(
-        dot_[block, rows, :].astype(jnp.float32) * attended.astype(jnp.float32), axis=0, keepdims=True
-    )
-    score_grads = [
-        (p * (g - delta)).astype(jnp.bfloat16) for p, g in zip(probs, prob_grad)
-    ]
-    graded = jnp.concatenate(score_grads, axis=0)
-    query_grad = dot(jnp.concatenate([kt[n, rows, :] for n in listed], axis=1), graded)
-    flipped[0, block, rows, :] = (query_grad * (1.0 / 8.0)).astype(jnp.bfloat16)
-    flipped[3, block, rows, :] = attended
-    value_part = dot(stacked, grad)
-    key_part = dot(graded, query)
-    for i, s in enumerate(starts):
-        value_acc[s, :] += value_part[i * BLK : (i + 1) * BLK]
-        key_acc[s, :] += key_part[i * BLK : (i + 1) * BLK]
-
-
-def attention_kernel(offs, heads, turned, grads, flipped, key_acc, value_acc):
+    nothing = jnp.zeros((BLK, BLK), jnp.bfloat16)
+    state = []
+    for head, block, count, back in jobs:
+        listed, used = [block], [None]
+        for i in range(1, width):
+            listed.append(jnp.maximum(block - back[i - 1], 0))
+            used.append(count >= i)
+        mine = (lanes >= HD) if head else (lanes < HD)
+        query = jnp.where(mine, q[rows_of(block), :], nothing)
+        grad = jnp.where(mine, do[rows_of(block), :], nothing)
+        both = jnp.concatenate(
+            [jnp.concatenate([query, nothing], axis=1), jnp.concatenate([nothing, grad], axis=1)],
+            axis=0,
+        )
+        pairs = jnp.concatenate(
+            [jnp.concatenate([grad, nothing], axis=1), jnp.concatenate([nothing, query], axis=1)],
+            axis=0,
+        )
+        state.append(dict(head=head, block=block, listed=listed, used=used, both=both, pairs=pairs))
+    for s in state:
+        left = jnp.concatenate(
+            [
+                jnp.concatenate([k[rows_of(n), :] for n in s["listed"]], axis=0),
+                jnp.concatenate([v[rows_of(n), :] for n in s["listed"]], axis=0),
+            ],
+            axis=1,
+        )
+        r = dot_nt(left, s["both"])
+        s["scores"] = [r[i * BLK : (i + 1) * BLK, :BLK] for i in range(width)]
+        s["prob_grad"] = [r[i * BLK : (i + 1) * BLK, BLK:] for i in range(width)]
+    for s in state:
+        scores = s["scores"]
+        scores[0] = jnp.where(key_at <= lanes, scores[0], -jnp.inf)
+        tops = [jnp.max(x, axis=0, keepdims=True) for x in scores]
+        top = tops[0]
+        for t, u in zip(tops[1:], s["used"][1:]):
+            top = jnp.maximum(top, jnp.where(u, t, -jnp.inf))
+        s["shift"] = [
+            top if u is None else jnp.where(u, top, jnp.inf) for u in s["used"]
+        ]
+    for s in state:
+        raised = [jnp.exp((x - t) * (1.0 / 8.0)) for x, t in zip(s["scores"], s["shift"])]
+        total, weighted = raised[0], raised[0] * s["prob_grad"][0]
+        for e, g in zip(raised[1:], s["prob_grad"][1:]):
+            total = total + e
+            weighted = weighted + e * g
+        share = 1.0 / jnp.sum(total, axis=0, keepdims=True)
+        delta = jnp.sum(weighted, axis=0, keepdims=True) * share
+        probs = [e * share for e in raised]
+        s["halves"] = [p.astype(jnp.bfloat16) for p in probs]
+        s["graded"] = [
+            (p * (g - delta)).astype(jnp.bfloat16) for p, g in zip(probs, s["prob_grad"])
+        ]
+    for s in state:
+        mine = pl.ds(s["head"] * HD, HD)
+        attended = dot(
+            jnp.concatenate([vt[n, mine, :] for n in s["listed"]], axis=1),
+            jnp.concatenate(s["halves"], axis=0),
+        )
+        query_grad = dot(
+            jnp.concatenate([kt[n, mine, :] for n in s["listed"]], axis=1),
+            jnp.concatenate(s["graded"], axis=0),
+        )
+        flipped[0, s["block"], mine, :] = (query_grad * (1.0 / 8.0)).astype(jnp.bfloat16)
+        flipped[3, s["block"], mine, :] = attended.astype(jnp.bfloat16)
+        left = jnp.concatenate(
+            [jnp.concatenate(s["halves"], axis=0), jnp.concatenate(s["graded"], axis=0)], axis=1
+        )
+        r = dot(left, s["pairs"])
+        s["parts"] = [r[i * BLK : (i + 1) * BLK] for i in range(width)]
+    for s, t in zip(state[::2], state[1::2]):
+        acc[rows_of(s["block"]), :] = s["parts"][0] + t["parts"][0]
+    for s in state:
+        homes = [
+            rows_of(jnp.where(u, n, blocks + i))
+            for i, (n, u) in enumerate(zip(s["listed"][1:], s["used"][1:]))
+        ]
+        sums = [acc[at, :] + part for at, part in zip(homes, s["parts"][1:])]
+        for at, new in zip(homes, sums):
+            acc[at, :] = new
+
+
+def attention_kernel(
+    offs, heads_h, turned_h, grads_h, flipped_h, heads, turned, grads, flipped, acc, load, save
+):
     q, k, v, do = (heads.at[n] for n in range(4))
-    kt, vt, dot_ = (turned.at[n] for n in range(3))
-    blocks = heads.shape[1] // BLK
-    key_acc[...] = jnp.zeros_like(key_acc)
-    value_acc[...] = jnp.zeros_like(value_acc)
-
-    @pl.loop(0, blocks)
-    def _(block):
-        for head in range(HEADS):
-            o1 = offs[head, block * 4 + 1]
-            o2 = offs[head, block * 4 + 2]
-            o3 = offs[head, block * 4 + 3]
-            v1 = (o1 <= block).astype(jnp.int32)
-            v2 = (o2 <= block).astype(jnp.int32)
-            v3 = (o3 <= block).astype(jnp.int32)
-            count = v1 + v2 + v3
-            first = jnp.where(v1 == 1, o1, jnp.where(v2 == 1, o2, o3))
-            second = jnp.where(v1 + v2 == 2, o2, o3)
-            for extra in range(4):
-                picked = [block] + [
-                    jnp.maximum(block - o, 0) for o in (first, second, o3)[:extra]
-                ]
-
-                @pl.when(count == extra)
-                def _(picked=picked, head=head):
-                    attend_head(
-                        head, block, picked, q, k, v, do, kt, vt, dot_, key_acc, value_acc, flipped
-                    )
-
-    @pl.loop(0, blocks)
-    def _(block):
-        own = pl.ds(pl.multiple_of(block * BLK, BLK), BLK)
-        grads[0, own, :] = flipped[0, block].T
-        kg = (key_acc[own, :] * (1.0 / 8.0)).astype(jnp.bfloat16)
-        vg = value_acc[own, :].astype(jnp.bfloat16)
-        grads[1, own, :] = kg
-        grads[2, own, :] = vg
-        flipped[1, block] = kg.T
-        flipped[2, block] = vg.T
+    kt, vt = (turned.at[n] for n in range(2))
+    blocks = turned.shape[1]
+    steps = blocks // GROUP
+    each = blocks // PIECES
+
+    def loads(piece):
+        rows = pl.ds(pl.multiple_of(piece * each * BLK, each * BLK), each * BLK)
+        some = pl.ds(piece * each, each)
+        return (
+            pltpu.make_async_copy(heads_h.at[:, rows], heads.at[:, rows], load.at[0, piece]),
+            pltpu.make_async_copy(turned_h.at[:, some], turned.at[:, some], load.at[1, piece]),
+        )
+
+    for piece in range(PIECES):
+        for item in loads(piece):
+            item.start()
+
+    def flipped_out(n, first, count):
+        at = pl.ds(first, count)
+        return pltpu.make_async_copy(flipped.at[n, at], flipped_h.at[n, at], save.at[n])
+
+    def grads_out(n, first, count):
+        at = pl.ds(pl.multiple_of(first * BLK, BLK), count * BLK)
+        return pltpu.make_async_copy(grads.at[n, at], grads_h.at[n, at], save.at[4 + n])
+
+    @pl.loop(0, steps)
+    def _(step):
+        @pl.when(step % (steps // PIECES) == 0)
+        def _():
+            for item in loads(step // (steps // PIECES)):
+                item.wait()
+
+        jobs, most = [], None
+        for g in range(GROUP):
+            for head in range(HEADS):
+                block = step * GROUP + g
+                count, back = slots_of(offs, head, block)
+                jobs.append((head, block, count, back))
+                most = count if most is None else jnp.maximum(most, count)
+        for extra in range(4):
+
+            @pl.when(most == extra)
+            def _(extra=extra):
+                attend(jobs, 1 + extra, blocks, q, k, v, do, kt, vt, acc, flipped)
+
+        for g in range(GROUP):
+            block = step * GROUP + g
+            grads[0, rows_of(block), :] = flipped[0, block].T
+        flipped_out(0, step * GROUP, GROUP).start()
+        flipped_out(3, step * GROUP, GROUP).start()
+        grads_out(0, step * GROUP, GROUP).start()
+
+    @pl.loop(0, PIECES)
+    def _(piece):
+        @pl.loop(0, each)
+        def _(i):
+            block = piece * each + i
+            own = rows_of(block)
+            both = acc[own, :]
+            vg = both[:, :BLK].astype(jnp.bfloat16)
+            kg = (both[:, BLK:] * (1.0 / 8.0)).astype(jnp.bfloat16)
+            grads[1, own, :] = kg
+            grads[2, own, :] = vg
+            flipped[1, block] = kg.T
+            flipped[2, block] = vg.T
+
+        for n in (1, 2):
+            grads_out(n, piece * each, each).start()
+            flipped_out(n, piece * each, each).start()
+
+    for n in range(4):
+        flipped_out(n, 0, blocks).wait()
+    for n in range(3):
+        grads_out(n, 0, blocks).wait()
 
 
 def attention(offsets, heads, turned):
     length, width = heads.shape[1:]
     blocks = length // BLK
-    whole = pl.BlockSpec(memory_space=pltpu.VMEM)
+    anywhere = pl.BlockSpec(memory_space=pl.ANY)
+    bf16 = jnp.bfloat16
     return pl.pallas_call(
         attention_kernel,
         out_shape=(
-            jax.ShapeDtypeStruct((3, length, width), jnp.bfloat16),
-            jax.ShapeDtypeStruct((4, blocks, width, BLK), jnp.bfloat16),
+            jax.ShapeDtypeStruct((3, length, width), bf16),
+            jax.ShapeDtypeStruct((4, blocks, width, BLK), bf16),
         ),
-        in_specs=[pl.BlockSpec(memory_space=pltpu.SMEM)] + [whole] * 2,
-        out_specs=(whole, whole),
+        in_specs=[pl.BlockSpec(memory_space=pltpu.SMEM)] + [anywhere] * 2,
+        out_specs=(anywhere, anywhere),
         scratch_shapes=[
-            pltpu.VMEM((length, width), jnp.float32),
-            pltpu.VMEM((length, width), jnp.float32),
+            pltpu.VMEM((4, length, width), bf16),
+            pltpu.VMEM((2, blocks, width, BLK), bf16),
+            pltpu.VMEM((3, length, width), bf16),
+            pltpu.VMEM((4, blocks, width, BLK), bf16),
+            pltpu.VMEM(((blocks + 3) * BLK, 2 * width), jnp.float32),
+            pltpu.SemaphoreType.DMA((2, PIECES)),
+            pltpu.SemaphoreType.DMA((7,)),
         ],
-        compiler_params=pltpu.CompilerParams(vmem_limit_bytes=48 << 20),
+        compiler_params=pltpu.CompilerParams(vmem_limit_bytes=60 << 20),
         cost_estimate=pl.CostEstimate(flops=4 << 30, bytes_accessed=12 << 20, transcendentals=3 << 20),
         name="attention",
     )(offsets.reshape(HEADS, -1), heads, turned)
@@ -219,8 +319,6 @@
             else:
                 part = dot_nt(x, w_back[...]).astype(jnp.bfloat16)
                 heads_v[3, at, :] = part
-                for i in range(3):
-                    flipped_v[2, chunk * 3 + i] = part[i * BLK : (i + 1) * BLK].T
 
     mine = pl.ds(pl.multiple_of(own * WIDTH, WIDTH), WIDTH)
     start_own(0)
@@ -258,20 +356,16 @@
         pltpu.make_async_copy(
             heads_v.at[pl.ds(first, count)], heads.at[pl.ds(first, count)], save.at[2 + a]
         ).start()
-        first, count = (0, 2) if a == 0 else (2, 1)
-        pltpu.make_async_copy(
-            flipped_v.at[pl.ds(first, count)], flipped.at[pl.ds(first, count)], save.at[4 + a]
-        ).start()
+        if a == 0:
+            pltpu.make_async_copy(flipped_v, flipped, save.at[4]).start()
     for a in range(2):
         pltpu.make_async_copy(land.at[a], rows_all.at[a], save.at[a]).wait()
         first, count = (0, 3) if a == 0 else (3, 1)
         pltpu.make_async_copy(
             heads_v.at[pl.ds(first, count)], heads.at[pl.ds(first, count)], save.at[2 + a]
         ).wait()
-        first, count = (0, 2) if a == 0 else (2, 1)
-        pltpu.make_async_copy(
-            flipped_v.at[pl.ds(first, count)], flipped.at[pl.ds(first, count)], save.at[4 + a]
-        ).wait()
+        if a == 0:
+            pltpu.make_async_copy(flipped_v, flipped, save.at[4]).wait()
         for slot, chunk, part in (
             (0, own, upper), (1, own, lower), (2, 2 * left + c, upper),
             (3, own, lower), (4, own, upper), (5, 2 * right + c, lower),
@@ -292,7 +386,7 @@
         out_shape=(
             jax.ShapeDtypeStruct((2, CHUNKS, ROWS, D), bf16),
             jax.ShapeDtypeStruct((4, length, WIDTH), bf16),
-            jax.ShapeDtypeStruct((3, blocks, BLK, BLK), bf16),
+            jax.ShapeDtypeStruct((2, blocks, BLK, BLK), bf16),
         ),
         in_specs=[anywhere] * 6,
         out_specs=(anywhere,) * 3,
@@ -301,7 +395,7 @@
             pltpu.VMEM((3, D, WIDTH), bf16),
             pltpu.VMEM((WIDTH, D), bf16),
             pltpu.VMEM((4, length, WIDTH), bf16),
-            pltpu.VMEM((3, blocks, BLK, BLK), bf16),
+            pltpu.VMEM((2, blocks, BLK, BLK), bf16),
             pltpu.SemaphoreType.DMA((2, 13)),
             pltpu.SemaphoreType.DMA((2, 13)),
             pltpu.SemaphoreType.DMA((6,)),
@@ -320,7 +414,7 @@
 def return_kernel(
     norm, rows_all, grads, flipped, w_query, w_key, w_value, grad_hidden, grad_weights,
     rows_v, flipped_v, w_v, back, out_acc, back_part, part_acc, part, x_in, z_out, z_in,
-    y_send, y_recv, o_send, o_recv, x_send, x_recv, z_send, z_recv, load,
+    y_send, y_recv, via, v_send, v_recv, f_send, o_send, o_recv, x_send, x_recv, z_send, z_recv, load,
 ):
     y, c = lax.axis_index("seq_0"), lax.axis_index("seq_1")
     x, z = lax.axis_index("batch_0"), lax.axis_index("batch_1")
@@ -357,6 +451,26 @@
             send_sem=y_send.at[a, 0], recv_sem=y_recv.at[a, chunk],
             device_id=peers[0], device_id_type=pl.DeviceIdType.MESH,
         ).wait_recv()
+
+    beside = ((y + 1) % 4, (y + 3) % 4)
+
+    def far_copy(a, side):
+        return remote(
+            grads.at[a, rows(2 * ((y + 2) % 4) + side)], via.at[side, a],
+            v_send.at[a, side], v_recv.at[a, side], seq_0=beside[side], seq_1=c,
+        )
+
+    def pass_on(a, side):
+        source = 2 * beside[1 - side] + c
+        return remote(
+            via.at[side, a], back.at[a, :, lanes(source)],
+            f_send.at[a, side], y_recv.at[a, source], seq_0=beside[side], seq_1=side,
+        )
+
+    def relay(a):
+        for side in range(2):
+            far_copy(a, side).wait_recv()
+            pass_on(a, side).start()
 
     loads = [
         pltpu.make_async_copy(rows_all.at[1], rows_v.at[1], load.at[0]),
@@ -371,7 +485,10 @@
     ]
     for item in loads[:2]:
         item.start()
-    for i in range(7):
+    for a in (2, 1, 0):
+        for side in range(2):
+            far_copy(a, side).start()
+    for i in range(5):
         y_copy(2, i).start()
     for item in loads[2:]:
         item.start()
@@ -405,8 +522,9 @@
 
     for i in range(7):
         o_copy(i).start()
+    relay(2)
     for a in (1, 0):
-        for i in range(7):
+        for i in range(5):
             y_copy(a, i).start()
     part[3, lanes(own), :] = back_part[:, lanes(own)]
 
@@ -447,6 +565,8 @@
 
     for i in range(3):
         x_copy(0, i).start()
+    relay(1)
+    relay(0)
     for item in loads[3:]:
         item.wait()
 
@@ -518,13 +638,15 @@
     grad_hidden[...] = (out_acc[...] + total).astype(jnp.bfloat16)
 
     for i in range(7):
-        for a in range(3):
+        for a in range(3 if i < 5 else 0):
             y_copy(a, i).wait_send()
         o_copy(i).wait_send()
         z_copy(i).wait_send()
     for i in range(3):
         for k in range(2):
             x_copy(k, i).wait_send()
+            far_copy(i, k).wait_send()
+            pass_on(i, k).wait_send()
 
 
 def hand_back(rows_all, grads, flipped, w_query, w_key, w_value, norm):
@@ -554,7 +676,8 @@
             pltpu.VMEM((4, 4, D // 4, WIDTH), bf16),
             pltpu.VMEM((4, D // 4, WIDTH), bf16),
             pltpu.VMEM((8, 4, 32, WIDTH), bf16),
-            dma((3, 7)), dma((3, 8)), dma((7,)), dma((8,)),
+            dma((3, 5)), dma((3, 8)), pltpu.VMEM((2, 3, ROWS, WIDTH), bf16),
+            dma((3, 2)), dma((3, 2)), dma((3, 2)), dma((7,)), dma((8,)),
             dma((2, 3)), dma((2, 4)), dma((7,)), dma((8,)), dma((9,)),
         ],
         compiler_params=pltpu.CompilerParams(

time: 150 us -> 129 us (0.86)
  Pallas kernels: 141 us -> 124 us
  local copies, waits for them, and re-layouts: 7.46 us -> 4.97 us
    pallas_call x1, Pallas kernels: 38.2 us -> 18.7 us  [attention(): pl.pallas_call(attention_kernel, out_shape=(jax.ShapeDtypeStruct((3, leng...]
    unnamed x7 -> x3, local copies, waits for them, and re-layouts: 7.36 us -> 4.31 us
    pallas_call x1, Pallas kernels: 41.9 us -> 44.3 us  [hand_back(): pl.pallas_call(functools.partial(return_kernel, norm), out_shape=(jax.Sha...]
where the time goes in v2:
time: 129 us
  Pallas kernels  124 us (96%)
  local copies, waits for them, and re-layouts  4.97 us (4%)
    pallas_call x1, Pallas kernels, gather(): pl.pallas_call(gather_kernel, out_shape=(jax.ShapeDtypeStruct((2, CHUNKS,...  60.7 us
    pallas_call x1, Pallas kernels, hand_back(): pl.pallas_call(functools.partial(return_kernel, norm), out_shape=(jax.Sha...  44.3 us
    pallas_call x1, Pallas kernels, attention(): pl.pallas_call(attention_kernel, out_shape=(jax.ShapeDtypeStruct((3, leng...  18.7 us
    unnamed x3, local copies, waits for them, and re-layouts  4.31 us

profile of v2, /device:TPU:1, one launch (start us, length us, event | category | flops | bytes accessed | tf_op | source)
XLA Modules:
  0.0 129.2 jit_solution(9736136338271359663)
XLA Ops:
  0.6 0.8 copy.10
  1.4 0.7 reshape_squeeze.3.offs
  2.1 60.7 %gather_and_project.1 = (bf16[2,8,384,1024]{3,2,1,0:T(8,128)(2,1)}, bf16[4,3072,128]{2,1,0:T(8,128)(2,1)}, bf16[2,24,128,128]{3,2,1,0:T(8,128)(2,1)}) custom-call(bf16[384,1024]{1,0:T(8,128)(2,1)} %bitcast.5, bf16[384,1024]{1,0:T(8,128)(2,1)} %bitcast.6, bf16[1024,1024]{1,0:T(8,128)(2,1)} %w_query.3, bf16[1024,1024]{1,0:T(8,128)(2,1)} %w_key.3, ...), custom_call_target="tpu_custom_call" | custom-call | tf_op jit(solution)/shard_map/gather_and_project/pallas_call | solution.py:384
  62.7 18.7 %attention.1 = (bf16[3,3072,128]{2,1,0:T(8,128)(2,1)}, bf16[4,24,128,128]{3,2,1,0:T(8,128)(2,1)}) custom-call(s32[2,96]{1,0:T(2,128)} %reshape_squeeze.3.offs, bf16[4,3072,128]{2,1,0:T(8,128)(2,1)} %get-tuple-element.10.heads_h, bf16[2,24,128,128]{3,2,1,0:T(8,128)(2,1)} %get-tuple-element.11.turned_h), custom_call_target="tpu_custom_call" | custom-call | flops 4294967296 | bytes 12582912 | tf_op jit(solution)/shard_map/attention/pallas_call | solution.py:211
  81.4 44.3 %return_and_reduce.1 = (bf16[384,1024]{1,0:T(8,128)(2,1)}, f32[4,32,128]{2,1,0:T(8,128)}) custom-call(bf16[2,8,384,1024]{3,2,1,0:T(8,128)(2,1)} %get-tuple-element.9.rows_all, bf16[3,3072,128]{2,1,0:T(8,128)(2,1)} %get-tuple-element.12.grads, bf16[4,24,128,128]{3,2,1,0:T(8,128)(2,1)} %get-tuple-element.13.flipped, bf16[1024,1024]{1,0:T(8,128)(2,1)} %w_query.3, ...), custom_call_target="tpu_custom_call" | custom-call | tf_op jit(solution)/shard_map/return_and_reduce/pallas_call | solution.py:659
  125.7 2.1 %copy.13 = bf16[1,384,1024]{2,1,0:T(8,128)(2,1)} copy(bf16[1,384,1024]{2,1,0:T(8,128)(2,1)} %bitcast.7) | data formatting | bytes 1572864
  127.8 1.5 %copy.14 = f32[4,32,128]{2,1,0:T(8,128)} copy(f32[4,32,128]{2,1,0:T(8,128)} %get-tuple-element.19) | data formatting | bytes 131072
